TPU v7x, 32 devices: a whole 2x2x4 slice. The times are simulated.
32 devices in a mesh: grp: 2 (over y), dev: 16 (over z, x, core).
Axes of the slice: x: 2, y: 2, z: 4, core: 2. Of those that a mesh axis runs over, the one named last changes fastest.
Arguments:
- queries: float32 [128, 1024], P(('grp', 'dev')), may hold values from -4.5 to 4.5
- documents: float32 [4096, 1024], P(('grp', 'dev')), may hold values from -0.75 to 0.75
- doc_codes: int32 [4096, 128], P(('grp', 'dev')), may hold values from 0 to 255
- codebook: float32 [256, 1024], replicated, may hold values from -0.75 to 0.75
- candidate_owner: int32 [128, 32], P(('grp', 'dev')), may hold values from 0 to 31, all different within a row; in each aligned block of 4 rows (0 to 3, 4 to 7, ...) at most 4 rows name the same one
- candidate_local: int32 [128, 32], P(('grp', 'dev')), may hold values from 0 to 127
Outputs:
- codebook_gradient: float32 [256, 1024], P('dev', 'grp')
- query_loss: float32 [128], P(('grp', 'dev'))
Inputs may be any that keep to these rules, and one draw needn't show every extreme that they name: `candidate_owner`: each query names 32 different owners; among one device's 4 queries no owner is named more than 4 times, and in some device's queries one owner is named exactly 4 times.
All inputs are finite; a program needn't handle non-finite values.
Results may differ from a plain program's by a relative error of at most 0.0003.
Values sent between devices are 32-bit elements; how exact they have to be, the bound alone decides.
No kernel may reach another device: no remote copies, remote signals or barrier semaphores. Data moves between devices by JAX's collectives and lax.ppermute only.
A program may use at most 192 MiB of HBM per device.

v0:
```python
import jax
import jax.numpy as jnp
from jax import lax
from jax.sharding import PartitionSpec as P

D = 1024
M = 128
K = 256
C = 32
SUB = 8


def slot_positions(candidate_owner, capacity):
    owner_flat = candidate_owner.reshape(-1)
    ordinal = jnp.arange(owner_flat.shape[0], dtype=jnp.int32)
    earlier = (owner_flat[None, :] == owner_flat[:, None]) & (ordinal[None, :] < ordinal[:, None])
    rank_inside = jnp.sum(earlier.astype(jnp.int32), axis=1)
    return owner_flat * capacity + rank_inside


def distill(exact_score, student):
    teacher = jax.nn.softmax(exact_score, axis=-1)
    query_loss = jnp.sum(
        teacher * (jax.nn.log_softmax(exact_score, axis=-1) - jax.nn.log_softmax(student, axis=-1)),
        axis=-1,
    )
    weight = jax.nn.softmax(student, axis=-1) - teacher
    return (query_loss, weight)


def code_onehot(code_block):
    return (code_block[:, :, None] == jnp.arange(K, dtype=jnp.int32)[None, None, :]).astype(
        jnp.float32
    )


def fetched_terms(queries, vectors, code_rows, codebook):
    query_count = queries.shape[0]
    exact_score = jnp.einsum("qcd,qd->qc", vectors, queries, precision=lax.Precision.HIGHEST)
    query_parts = queries.reshape(query_count, M, SUB)
    lookup = jnp.einsum(
        "qmj,kmj->qmk", query_parts, codebook.reshape(K, M, SUB), precision=lax.Precision.HIGHEST
    )

    def student_one(pieces):
        code_one, lookup_one = pieces
        return jnp.einsum(
            "cmk,mk->c", code_onehot(code_one), lookup_one, precision=lax.Precision.HIGHEST
        )

    student = lax.map(student_one, (code_rows, lookup))
    query_loss, weight = distill(exact_score, student)

    def table_one(pieces):
        code_one, weight_one = pieces
        return jnp.einsum(
            "cmk,c->mk", code_onehot(code_one), weight_one, precision=lax.Precision.HIGHEST
        )

    weight_table = lax.map(table_one, (code_rows, weight))
    gradient = jnp.einsum(
        "qmk,qmj->kmj", weight_table, query_parts, precision=lax.Precision.HIGHEST
    )
    return (query_loss, gradient.reshape(K, D))


def shards(queries, documents, doc_codes, codebook, candidate_owner, candidate_local):
    groups = lax.axis_size("grp")
    owners = lax.axis_size("dev")
    query_count = queries.shape[0]
    capacity = min(query_count, max(2, 2 * query_count * C // (groups * owners)))
    slot_count = groups * owners * capacity
    positions = slot_positions(candidate_owner, capacity)
    wanted = jnp.zeros((slot_count,), jnp.int32).at[positions].set(candidate_local.reshape(-1))
    asked = lax.all_to_all(
        lax.all_to_all(
            wanted.reshape(groups, owners, capacity), "grp", split_axis=0, concat_axis=0, tiled=True
        ),
        "dev",
        split_axis=1,
        concat_axis=1,
        tiled=True,
    )
    doc_index = asked.reshape(slot_count)
    found_rows = documents[doc_index].reshape(groups, owners, capacity, D)
    found_codes = doc_codes[doc_index].astype(jnp.float32).reshape(groups, owners, capacity, M)
    fetched, fetched_codes = (
        lax.all_to_all(
            lax.all_to_all(found_rows, "grp", split_axis=0, concat_axis=0, tiled=True),
            "dev",
            split_axis=1,
            concat_axis=1,
            tiled=True,
        ),
        lax.all_to_all(
            lax.all_to_all(found_codes, "grp", split_axis=0, concat_axis=0, tiled=True),
            "dev",
            split_axis=1,
            concat_axis=1,
            tiled=True,
        ),
    )
    vectors = fetched.reshape(slot_count, D)[positions].reshape(query_count, C, D)
    code_rows = (
        fetched_codes.reshape(slot_count, M)[positions].astype(jnp.int32).reshape(query_count, C, M)
    )
    query_loss, local_gradient = fetched_terms(queries, vectors, code_rows, codebook)
    partial_sum = lax.psum_scatter(local_gradient, "dev", scatter_dimension=0, tiled=True)
    codebook_gradient = lax.psum_scatter(partial_sum, "grp", scatter_dimension=1, tiled=True)
    return (codebook_gradient, query_loss)


def solution(mesh):
    in_specs = (
        P(("grp", "dev"), None),
        P(("grp", "dev"), None),
        P(("grp", "dev"), None),
        P(),
        P(("grp", "dev"), None),
        P(("grp", "dev"), None),
    )
    out_specs = (P("dev", "grp"), P(("grp", "dev")))
    return jax.shard_map(shards, mesh=mesh, in_specs=in_specs, out_specs=out_specs, check_vma=False)
```

profile of v0, /device:TPU:0, one launch (start us, length us, event | category | flops | bytes accessed | tf_op | source)
XLA Modules:
  0.0 180.2 jit_solution(6461381742338682574)
XLA Ops:
  7.2 0.8 broadcast_multiply_fusion
  8.0 0.8 eq.45
  8.8 0.1 mul.21
  8.8 0.2 convert_reduce_fusion
  9.0 0.8 reshape.158
  9.8 1.0 scatter_custom_fusion
  10.8 0.1 reshape.113
  10.9 0.1 copy.46
  11.0 7.8 %all_to_all.30 = s32[2,16,4]{1,2,0:T(4,128)S(1)} all-to-all(s32[2,16,4]{1,2,0:T(4,128)S(1)} %copy.46), channel_id=1, replica_groups=mesh['grp'=2,'dev'=16] {'grp'}, dimensions={0} | all-to-all | bytes 1024 | tf_op jit(solution)/shard_map/all_to_all | solution.py:76
  18.8 0.1 copy.47
  18.9 12.2 %all_to_all.31 = s32[2,16,4]{2,0,1:T(2,128)S(1)} all-to-all(s32[2,16,4]{2,0,1:T(2,128)S(1)} %copy.47), channel_id=1, replica_groups=mesh['grp'=2,'dev'=16] {'dev'}, dimensions={1} | all-to-all | bytes 1024 | tf_op jit(solution)/shard_map/all_to_all | solution.py:75
  31.1 0.1 reshape.114
  31.2 1.5 gather_fusion
  32.7 6.5 %all_to_all.32 = f32[2,16,4,128]{3,2,1,0:T(4,128)S(1)} all-to-all(f32[2,16,4,128]{3,2,1,0:T(4,128)S(1)} %bitcast.63), channel_id=1, replica_groups=mesh['grp'=2,'dev'=16] {'grp'}, dimensions={0} | all-to-all | bytes 131072 | tf_op jit(solution)/shard_map/all_to_all | solution.py:96
  39.2 0.6 copy.49
  39.8 3.5 %all-to-all-start.3 = ((f32[2,16,4,128]{3,2,0,1:T(4,128)}), f32[2,16,4,128]{3,2,0,1:T(4,128)S(1)}, u32[]{:S(2)}, u32[]{:S(2)}) async-start(f32[2,16,4,128]{3,2,0,1:T(4,128)} %copy.49), calls=%async_computation.3 | async-start | bytes 131072 | tf_op jit(solution)/shard_map/all_to_all | solution.py:95
  43.4 0.2 reshape.117
  43.5 0.3 copy.51
  43.9 0.8 gather_fusion.2
  44.7 1.0 reshape.118
  45.7 4.5 %all-to-all-done.3 = f32[2,16,4,128]{3,2,0,1:T(4,128)S(1)} async-done(((f32[2,16,4,128]{3,2,0,1:T(4,128)}), f32[2,16,4,128]{3,2,0,1:T(4,128)S(1)}, u32[]{:S(2)}, u32[]{:S(2)}) %all-to-all-start.3) | async-done | bytes 65568 | tf_op jit(solution)/shard_map/all_to_all | solution.py:95
  50.2 3.5 %all-to-all-start.4 = ((f32[2,16,4,1024]{3,2,1,0:T(4,128)}), f32[2,16,4,1024]{3,2,1,0:T(4,128)S(1)}, u32[]{:S(2)}, u32[]{:S(2)}) async-start(f32[2,16,4,1024]{3,2,1,0:T(4,128)} %reshape.118), calls=%async_computation.4 | async-start | bytes 1048576 | tf_op jit(solution)/shard_map/all_to_all | solution.py:89
  53.7 1.1 convolution_bitcast_fusion.1
  54.9 0.6 gather_fusion.1
  55.5 6.1 %all-to-all-done.4 = f32[2,16,4,1024]{3,2,1,0:T(4,128)S(1)} async-done(((f32[2,16,4,1024]{3,2,1,0:T(4,128)}), f32[2,16,4,1024]{3,2,1,0:T(4,128)S(1)}, u32[]{:S(2)}, u32[]{:S(2)}) %all-to-all-start.4) | async-done | bytes 524320 | tf_op jit(solution)/shard_map/all_to_all | solution.py:89
  61.7 0.9 copy.54
  62.5 3.6 %all-to-all-start.5 = ((f32[2,16,4,1024]{3,2,0,1:T(4,128)}), f32[2,16,4,1024]{3,2,0,1:T(4,128)S(1)}, u32[]{:S(2)}, u32[]{:S(2)}) async-start(f32[2,16,4,1024]{3,2,0,1:T(4,128)} %copy.54), calls=%async_computation.5 | async-start | bytes 1048576 | tf_op jit(solution)/shard_map/all_to_all | solution.py:88
  66.1 0.0 reduce-scatter.3.cloned.1.call-start
  66.1 6.7 %while.20 = (s32[]{:T(128)}, f32[4,32]{1,0:T(4,128)S(1)}, s32[4,32,128]{2,1,0:T(8,128)S(1)}, f32[4,128,256]{2,0,1:T(4,128)S(1)}, s32[]{:T(128)}, /*index=5*/s32[]{:T(128)}) while((s32[]{:T(128)}, f32[4,32]{1,0:T(4,128)S(1)}, s32[4,32,128]{2,1,0:T(8,128)S(1)}, f32[4,128,256]{2,0,1:T(4,128)S(1)}, s32[]{:T(128)}, /*index=5*/s32[]{:T(128)}) %tuple.53), condition=%wide.region_3.4_spmd, body=%wide.region_2.3_spmd.sunk | while | flops 3145698 | bytes 704977 | solution.py:51
  66.2 0.1 constant_dynamic-slice_fusion.2
  66.3 1.5 select_reduce_fusion.2
  67.8 0.1 constant_dynamic-slice_fusion.2
  68.0 1.5 select_reduce_fusion.2
  69.5 0.1 constant_dynamic-slice_fusion.2
  69.7 1.5 select_reduce_fusion.2
  71.2 0.1 constant_dynamic-slice_fusion.2
  71.4 1.5 select_reduce_fusion.2
  72.9 0.1 reduce_max.27
  73.0 7.5 %all-to-all-done.5 = f32[2,16,4,1024]{3,2,0,1:T(4,128)S(1)} async-done(((f32[2,16,4,1024]{3,2,0,1:T(4,128)}), f32[2,16,4,1024]{3,2,0,1:T(4,128)S(1)}, u32[]{:S(2)}, u32[]{:S(2)}) %all-to-all-start.5) | async-done | bytes 524320 | tf_op jit(solution)/shard_map/all_to_all | solution.py:88
  80.6 0.2 reshape.119
  80.8 0.8 gather_fusion.3
  81.6 0.6 fusion.8
  82.1 0.1 reduce_max.28
  82.2 0.2 exponential_reduce_fusion
  82.5 0.7 fusion.11
  83.2 19.7 %while.21 = (s32[]{:T(128)}, f32[4,128,256]{2,0,1:T(4,128)S(1)}, s32[4,32,128]{2,1,0:T(8,128)S(1)}, f32[4,32]{1,0:T(4,128)S(1)}, s32[]{:T(128)}, /*index=5*/s32[]{:T(128)}) while((s32[]{:T(128)}, f32[4,128,256]{2,0,1:T(4,128)S(1)}, s32[4,32,128]{2,1,0:T(8,128)S(1)}, f32[4,32]{1,0:T(4,128)S(1)}, s32[]{:T(128)}, /*index=5*/s32[]{:T(128)}) %tuple.55), condition=%wide.region_9.10_spmd, body=%wide.region_8.9_spmd.sunk | while | flops 13631490 | bytes 2540113 | solution.py:60
  83.2 0.8 iota_compare_fusion.4
  84.1 2.2 %fusion.21 = f32[1,128,256]{2,0,1:T(1,128)S(1)} fusion(pred[32,128,256]{2,1,0:T(32,128)(4,1)S(1)} %iota_compare_fusion.4, f32[4,32]{1,0:T(4,128)S(1)} %get-tuple-element.172, s32[]{:T(128)} %get-tuple-element.163), kind=kOutput, calls=%fused_computation.6.clone.1 | convolution fusion | flops 12582912 | bytes 1180164 | tf_op jit(solution)/shard_map/while/body/eval_jaxpr/cmk,c->mk/dot_general | solution.py:56
  86.2 1.8 %dynamic_update_slice.11 = f32[4,128,256]{2,0,1:T(4,128)S(1)} dynamic-update-slice(f32[4,128,256]{2,0,1:T(4,128)S(1)} %get-tuple-element.164, f32[1,128,256]{2,0,1:T(1,128)S(1)} %fusion.21, s32[]{:T(128)} %get-tuple-element.163, s32[]{:T(128)} %constant.21.clone.1..sunk.1, s32[]{:T(128)} %constant.21.clone.1..sunk.1) | dynamic-update-slice | bytes 262148 | tf_op jit(solution)/shard_map/while/body/jit(dynamic_update_index_in_dim)/dynamic_update_slice | solution.py:60
  88.1 0.9 iota_compare_fusion.4
  89.0 2.2 %fusion.21 = f32[1,128,256]{2,0,1:T(1,128)S(1)} fusion(pred[32,128,256]{2,1,0:T(32,128)(4,1)S(1)} %iota_compare_fusion.4, f32[4,32]{1,0:T(4,128)S(1)} %get-tuple-element.172, s32[]{:T(128)} %get-tuple-element.163), kind=kOutput, calls=%fused_computation.6.clone.1 | convolution fusion | flops 12582912 | bytes 1180164 | tf_op jit(solution)/shard_map/while/body/eval_jaxpr/cmk,c->mk/dot_general | solution.py:56
  91.2 1.8 %dynamic_update_slice.11 = f32[4,128,256]{2,0,1:T(4,128)S(1)} dynamic-update-slice(f32[4,128,256]{2,0,1:T(4,128)S(1)} %get-tuple-element.164, f32[1,128,256]{2,0,1:T(1,128)S(1)} %fusion.21, s32[]{:T(128)} %get-tuple-element.163, s32[]{:T(128)} %constant.21.clone.1..sunk.1, s32[]{:T(128)} %constant.21.clone.1..sunk.1) | dynamic-update-slice | bytes 262148 | tf_op jit(solution)/shard_map/while/body/jit(dynamic_update_index_in_dim)/dynamic_update_slice | solution.py:60
  93.1 0.9 iota_compare_fusion.4
  93.9 2.2 %fusion.21 = f32[1,128,256]{2,0,1:T(1,128)S(1)} fusion(pred[32,128,256]{2,1,0:T(32,128)(4,1)S(1)} %iota_compare_fusion.4, f32[4,32]{1,0:T(4,128)S(1)} %get-tuple-element.172, s32[]{:T(128)} %get-tuple-element.163), kind=kOutput, calls=%fused_computation.6.clone.1 | convolution fusion | flops 12582912 | bytes 1180164 | tf_op jit(solution)/shard_map/while/body/eval_jaxpr/cmk,c->mk/dot_general | solution.py:56
  96.1 1.8 %dynamic_update_slice.11 = f32[4,128,256]{2,0,1:T(4,128)S(1)} dynamic-update-slice(f32[4,128,256]{2,0,1:T(4,128)S(1)} %get-tuple-element.164, f32[1,128,256]{2,0,1:T(1,128)S(1)} %fusion.21, s32[]{:T(128)} %get-tuple-element.163, s32[]{:T(128)} %constant.21.clone.1..sunk.1, s32[]{:T(128)} %constant.21.clone.1..sunk.1) | dynamic-update-slice | bytes 262148 | tf_op jit(solution)/shard_map/while/body/jit(dynamic_update_index_in_dim)/dynamic_update_slice | solution.py:60
  98.0 0.9 iota_compare_fusion.4
  98.9 2.2 %fusion.21 = f32[1,128,256]{2,0,1:T(1,128)S(1)} fusion(pred[32,128,256]{2,1,0:T(32,128)(4,1)S(1)} %iota_compare_fusion.4, f32[4,32]{1,0:T(4,128)S(1)} %get-tuple-element.172, s32[]{:T(128)} %get-tuple-element.163), kind=kOutput, calls=%fused_computation.6.clone.1 | convolution fusion | flops 12582912 | bytes 1180164 | tf_op jit(solution)/shard_map/while/body/eval_jaxpr/cmk,c->mk/dot_general | solution.py:56
  101.0 1.8 %dynamic_update_slice.11 = f32[4,128,256]{2,0,1:T(4,128)S(1)} dynamic-update-slice(f32[4,128,256]{2,0,1:T(4,128)S(1)} %get-tuple-element.164, f32[1,128,256]{2,0,1:T(1,128)S(1)} %fusion.21, s32[]{:T(128)} %get-tuple-element.163, s32[]{:T(128)} %constant.21.clone.1..sunk.1, s32[]{:T(128)} %constant.21.clone.1..sunk.1) | dynamic-update-slice | bytes 262148 | tf_op jit(solution)/shard_map/while/body/jit(dynamic_update_index_in_dim)/dynamic_update_slice | solution.py:60
  102.9 1.4 convolution_bitcast_fusion
  104.3 1.3 copy.58
  105.6 0.0 reduce-scatter.3.cloned.1.call-update
  105.6 0.0 reduce-scatter.5.cloned.1.call-start
  105.7 55.9 %reduce-scatter.3.cloned.1.call-done = f32[16,1024]{1,0:T(8,128)} async-done(((f32[256,1024]{1,0:T(8,128)}), f32[16,1024]{1,0:T(8,128)}) %reduce-scatter.3.cloned.1.call-update) | async-done | bytes 65552 | tf_op jit(solution)/shard_map/reduce_scatter | solution.py:108
  161.6 11.7 %reduce-scatter.5.cloned.1.call-done = f32[16,512]{1,0:T(8,128)} async-done(((f32[16,1024]{1,0:T(8,128)}), f32[16,512]{1,0:T(8,128)}) %reduce-scatter.5.cloned.1.call-update) | async-done | bytes 32784 | tf_op jit(solution)/shard_map/reduce_scatter | solution.py:109
  (38 shorter events, 0.4 us)
Async XLA Ops:
  7.2 36.7 %copy-start = (f32[128,1024]{1,0:T(8,128)S(1)}, f32[128,1024]{1,0:T(8,128)}, u32[]{:S(2)}) copy-start(f32[128,1024]{1,0:T(8,128)} %param.12) | copy-start | bytes 1572868
  7.2 36.2 %copy-start.3 = (f32[4,1024]{1,0:T(4,128)S(1)}, f32[4,1024]{1,0:T(4,128)}, u32[]{:S(2)}) copy-start(f32[4,1024]{1,0:T(4,128)} %param.11) | copy-start | bytes 49156
  7.2 36.4 %copy-start.1 = (f32[256,1024]{1,0:T(8,128)S(1)}, f32[256,1024]{1,0:T(8,128)}, u32[]{:S(2)}) copy-start(f32[256,1024]{1,0:T(8,128)} %param.14) | copy-start | bytes 3145732
  39.8 10.4 %all-to-all-start.3 = ((f32[2,16,4,128]{3,2,0,1:T(4,128)}), f32[2,16,4,128]{3,2,0,1:T(4,128)S(1)}, u32[]{:S(2)}, u32[]{:S(2)}) async-start(f32[2,16,4,128]{3,2,0,1:T(4,128)} %copy.49), calls=%async_computation.3 | async-start | bytes 131072 | tf_op jit(solution)/shard_map/all_to_all | solution.py:95
  50.2 11.5 %all-to-all-start.4 = ((f32[2,16,4,1024]{3,2,1,0:T(4,128)}), f32[2,16,4,1024]{3,2,1,0:T(4,128)S(1)}, u32[]{:S(2)}, u32[]{:S(2)}) async-start(f32[2,16,4,1024]{3,2,1,0:T(4,128)} %reshape.118), calls=%async_computation.4 | async-start | bytes 1048576 | tf_op jit(solution)/shard_map/all_to_all | solution.py:89
  62.5 18.0 %all-to-all-start.5 = ((f32[2,16,4,1024]{3,2,0,1:T(4,128)}), f32[2,16,4,1024]{3,2,0,1:T(4,128)S(1)}, u32[]{:S(2)}, u32[]{:S(2)}) async-start(f32[2,16,4,1024]{3,2,0,1:T(4,128)} %copy.54), calls=%async_computation.5 | async-start | bytes 1048576 | tf_op jit(solution)/shard_map/all_to_all | solution.py:88
  66.1 95.5 %reduce-scatter.3.cloned.1.call-start = ((), (), s32[]{:S(2)}) async-start(), calls=%async_computation.8 | async-start | bytes 1114112 | tf_op jit(solution)/shard_map/reduce_scatter | solution.py:108
  80.7 2.5 %copy-start.2 = (f32[4,128,256]{2,0,1:T(4,128)S(1)}, f32[4,128,256]{2,0,1:T(4,128)}, u32[]{:S(2)}) copy-start(f32[4,128,256]{2,0,1:T(4,128)} %custom-call.9) | copy-start | bytes 1572868
  105.6 67.8 %reduce-scatter.5.cloned.1.call-start = ((), (), s32[]{:S(2)}) async-start(), calls=%async_computation.9 | async-start | bytes 98304 | tf_op jit(solution)/shard_map/reduce_scatter | solution.py:109
Sparse Core Ops, SparseCore 0:
  105.7 55.8 reduce-scatter.2
  164.5 8.8 reduce-scatter.4
where the time goes:
time: 181 us; the launch traced here: 180 us
  waiting for transfers between devices  85.9 us (47%)
  blocking collectives  26.5 us (15%)
  local copies, waits for them, and re-layouts  19.3 us (11%)
  between operations  14.3 us (8%)
  matrix products  11.8 us (7%)
  other arithmetic  11.6 us (6%)
  starting transfers between devices  10.6 us (6%)
    reduce_scatter x1, waiting for transfers between devices, shards(): lax.psum_scatter(local_gradient, 'dev', scatter_dimension=0, tiled=True)  55.9 us
    all_to_all x1, blocking collectives, shards(): lax.all_to_all(lax.all_to_all(wanted.reshape(groups, owners, capacity), '...  12.2 us
    reduce_scatter x1, waiting for transfers between devices, shards(): lax.psum_scatter(partial_sum, 'grp', scatter_dimension=1, tiled=True)  11.7 us
    dot_general x4, matrix products, table_one(): jnp.einsum('cmk,c->mk', code_onehot(code_one), weight_one, precision=lax....  8.72 us
    all_to_all x1, blocking collectives, shards(): lax.all_to_all(wanted.reshape(groups, owners, capacity), 'grp', split_axi...  7.82 us
    all_to_all x1, waiting for transfers between devices, shards(): lax.all_to_all(lax.all_to_all(found_rows, 'grp', split_axis=0, concat_axi...  7.51 us
    dynamic_update_slice x4, local copies, waits for them, and re-layouts, fetched_terms(): weight_table = lax.map(table_one, (code_rows, weight))  7.34 us
    all_to_all x1, blocking collectives, shards(): lax.all_to_all(found_codes, 'grp', split_axis=0, concat_axis=0, tiled=True)  6.5 us
  transfers between devices with their start and end apart: 5, of which 5 were waited for; matrix products, arithmetic and copies ran while one was open for 6% of the time, Pallas kernels for 0%

commit v1 on v0

--- a/solution.py
+++ b/solution.py
@@ -84,14 +84,14 @@
     doc_index = asked.reshape(slot_count)
     found_rows = documents[doc_index].reshape(groups, owners, capacity, D)
     found_codes = doc_codes[doc_index].astype(jnp.float32).reshape(groups, owners, capacity, M)
+    cube_spread = lambda local_array: jnp.concatenate(
+        lax.all_to_all(
+            jnp.stack(jnp.split(local_array, lax.axis_size("dev"), axis=1), axis=0), "dev", 0, 0
+        ),
+        axis=1,
+    )
     fetched, fetched_codes = (
-        lax.all_to_all(
-            lax.all_to_all(found_rows, "grp", split_axis=0, concat_axis=0, tiled=True),
-            "dev",
-            split_axis=1,
-            concat_axis=1,
-            tiled=True,
-        ),
+        cube_spread(lax.all_to_all(found_rows, "grp", split_axis=0, concat_axis=0, tiled=True)),
         lax.all_to_all(
             lax.all_to_all(found_codes, "grp", split_axis=0, concat_axis=0, tiled=True),
             "dev",

time: 181 us -> 190 us (1.050)
  local copies, waits for them, and re-layouts: 19.3 us -> 28.1 us
    unnamed x9 -> x24, local copies, waits for them, and re-layouts: 0.35 us -> 9.42 us
where the time goes in v1:
time: 190 us; the launch traced here: 189 us
  waiting for transfers between devices  85.9 us (45%)
  local copies, waits for them, and re-layouts  28.1 us (15%)
  blocking collectives  26.5 us (14%)
  between operations  14.3 us (8%)
  matrix products  11.8 us (6%)
  other arithmetic  11.6 us (6%)
  starting transfers between devices  10.6 us (6%)
    reduce_scatter x1, waiting for transfers between devices, shards(): lax.psum_scatter(local_gradient, 'dev', scatter_dimension=0, tiled=True)  55.9 us
    all_to_all x1, blocking collectives, shards(): lax.all_to_all(lax.all_to_all(wanted.reshape(groups, owners, capacity), '...  12.2 us
    reduce_scatter x1, waiting for transfers between devices, shards(): lax.psum_scatter(partial_sum, 'grp', scatter_dimension=1, tiled=True)  11.7 us
    unnamed x24, local copies, waits for them, and re-layouts  9.42 us
    dot_general x4, matrix products, table_one(): jnp.einsum('cmk,c->mk', code_onehot(code_one), weight_one, precision=lax....  8.72 us
    all_to_all x1, blocking collectives, shards(): lax.all_to_all(wanted.reshape(groups, owners, capacity), 'grp', split_axi...  7.82 us
    all_to_all x1, waiting for transfers between devices, shards(): lax.all_to_all(jnp.stack(jnp.split(local_array, lax.axis_size('dev'), axi...  7.51 us
    dynamic_update_slice x4, local copies, waits for them, and re-layouts, fetched_terms(): weight_table = lax.map(table_one, (code_rows, weight))  7.34 us
  transfers between devices with their start and end apart: 5, of which 5 were waited for; matrix products, arithmetic and copies ran while one was open for 6% of the time, Pallas kernels for 0%

profile of v1, /device:TPU:0, one launch (start us, length us, event | category | flops | bytes accessed | tf_op | source)
XLA Modules:
  0.0 189.0 jit_solution(4928389325548906509)
XLA Ops:
  7.2 0.8 broadcast_multiply_fusion
  8.0 0.8 eq.45
  8.8 0.2 convert_reduce_fusion
  9.0 0.8 reshape.158
  9.8 1.0 scatter_custom_fusion
  11.0 7.8 %all_to_all.30 = s32[2,16,4]{1,2,0:T(4,128)S(1)} all-to-all(s32[2,16,4]{1,2,0:T(4,128)S(1)} %copy.106), channel_id=1, replica_groups=mesh['grp'=2,'dev'=16] {'grp'}, dimensions={0} | all-to-all | bytes 1024 | tf_op jit(solution)/shard_map/all_to_all | solution.py:76
  18.9 12.2 %all_to_all.31 = s32[2,16,4]{2,0,1:T(2,128)S(1)} all-to-all(s32[2,16,4]{2,0,1:T(2,128)S(1)} %copy.107), channel_id=1, replica_groups=mesh['grp'=2,'dev'=16] {'dev'}, dimensions={1} | all-to-all | bytes 1024 | tf_op jit(solution)/shard_map/all_to_all | solution.py:75
  31.2 1.5 gather_fusion
  32.7 6.5 %all_to_all.32 = f32[2,16,4,128]{3,2,1,0:T(4,128)S(1)} all-to-all(f32[2,16,4,128]{3,2,1,0:T(4,128)S(1)} %bitcast.161), channel_id=1, replica_groups=mesh['grp'=2,'dev'=16] {'grp'}, dimensions={0} | all-to-all | bytes 131072 | tf_op jit(solution)/shard_map/all_to_all | solution.py:96
  39.2 0.6 copy.109
  39.8 3.5 %all-to-all-start.3 = ((f32[2,16,4,128]{3,2,0,1:T(4,128)}), f32[2,16,4,128]{3,2,0,1:T(4,128)S(1)}, u32[]{:S(2)}, u32[]{:S(2)}) async-start(f32[2,16,4,128]{3,2,0,1:T(4,128)} %copy.109), calls=%async_computation.3 | async-start | bytes 131072 | tf_op jit(solution)/shard_map/all_to_all | solution.py:95
  43.5 0.3 copy.111
  43.9 0.8 gather_fusion.2
  44.7 1.0 reshape.118
  45.7 4.5 %all-to-all-done.3 = f32[2,16,4,128]{3,2,0,1:T(4,128)S(1)} async-done(((f32[2,16,4,128]{3,2,0,1:T(4,128)}), f32[2,16,4,128]{3,2,0,1:T(4,128)S(1)}, u32[]{:S(2)}, u32[]{:S(2)}) %all-to-all-start.3) | async-done | bytes 65568 | tf_op jit(solution)/shard_map/all_to_all | solution.py:95
  50.2 3.5 %all-to-all-start.4 = ((f32[2,16,4,1024]{3,2,1,0:T(4,128)}), f32[2,16,4,1024]{3,2,1,0:T(4,128)S(1)}, u32[]{:S(2)}, u32[]{:S(2)}) async-start(f32[2,16,4,1024]{3,2,1,0:T(4,128)} %reshape.118), calls=%async_computation.4 | async-start | bytes 1048576 | tf_op jit(solution)/shard_map/all_to_all | solution.py:94
  53.7 1.1 convolution_bitcast_fusion.1
  54.9 0.6 gather_fusion.1
  55.5 6.1 %all-to-all-done.4 = f32[2,16,4,1024]{3,2,1,0:T(4,128)S(1)} async-done(((f32[2,16,4,1024]{3,2,1,0:T(4,128)}), f32[2,16,4,1024]{3,2,1,0:T(4,128)S(1)}, u32[]{:S(2)}, u32[]{:S(2)}) %all-to-all-start.4) | async-done | bytes 524320 | tf_op jit(solution)/shard_map/all_to_all | solution.py:94
  61.7 0.6 fusion.23
  62.3 0.6 fusion.22
  62.9 0.6 fusion.21
  63.5 0.6 fusion.20
  64.1 0.6 fusion.19
  64.7 0.6 fusion.18
  65.3 0.6 fusion.17
  65.9 0.6 fusion.16
  66.5 0.6 fusion.15
  67.1 0.6 fusion.14
  67.7 0.6 fusion.13
  68.3 0.6 fusion.12
  68.9 0.6 fusion.11
  69.5 0.6 fusion.10
  70.1 0.6 fusion.9
  70.7 0.6 fusion.8
  71.3 3.6 %all-to-all-start.5 = ((f32[16,2,1,4,1024]{4,3,1,2,0:T(4,128)}), f32[16,2,1,4,1024]{4,3,1,2,0:T(4,128)S(1)}, u32[]{:S(2)}, u32[]{:S(2)}) async-start(f32[16,2,1,4,1024]{4,3,1,2,0:T(4,128)} %fusion.8), calls=%async_computation.5 | async-start | bytes 1048576 | tf_op jit(solution)/shard_map/all_to_all | solution.py:88
  75.0 6.7 %while.20 = (s32[]{:T(128)}, f32[4,32]{1,0:T(4,128)S(1)}, s32[4,32,128]{2,1,0:T(8,128)S(1)}, f32[4,128,256]{2,0,1:T(4,128)S(1)}, s32[]{:T(128)}, /*index=5*/s32[]{:T(128)}) while((s32[]{:T(128)}, f32[4,32]{1,0:T(4,128)S(1)}, s32[4,32,128]{2,1,0:T(8,128)S(1)}, f32[4,128,256]{2,0,1:T(4,128)S(1)}, s32[]{:T(128)}, /*index=5*/s32[]{:T(128)}) %tuple.53), condition=%wide.region_3.4_spmd, body=%wide.region_2.3_spmd.sunk | while | flops 3145698 | bytes 704977 | solution.py:51
  75.1 1.5 select_reduce_fusion.2
  76.8 1.5 select_reduce_fusion.2
  78.5 1.5 select_reduce_fusion.2
  80.2 1.5 select_reduce_fusion.2
  81.8 7.5 %all-to-all-done.5 = f32[16,2,1,4,1024]{4,3,1,2,0:T(4,128)S(1)} async-done(((f32[16,2,1,4,1024]{4,3,1,2,0:T(4,128)}), f32[16,2,1,4,1024]{4,3,1,2,0:T(4,128)S(1)}, u32[]{:S(2)}, u32[]{:S(2)}) %all-to-all-start.5) | async-done | bytes 524320 | tf_op jit(solution)/shard_map/all_to_all | solution.py:88
  89.4 0.2 reshape_reshape.3
  89.6 0.8 gather_fusion.3
  90.4 0.6 fusion.24
  91.1 0.2 exponential_reduce_fusion
  91.3 0.7 fusion.27
  92.0 19.7 %while.21 = (s32[]{:T(128)}, f32[4,128,256]{2,0,1:T(4,128)S(1)}, s32[4,32,128]{2,1,0:T(8,128)S(1)}, f32[4,32]{1,0:T(4,128)S(1)}, s32[]{:T(128)}, /*index=5*/s32[]{:T(128)}) while((s32[]{:T(128)}, f32[4,128,256]{2,0,1:T(4,128)S(1)}, s32[4,32,128]{2,1,0:T(8,128)S(1)}, f32[4,32]{1,0:T(4,128)S(1)}, s32[]{:T(128)}, /*index=5*/s32[]{:T(128)}) %tuple.55), condition=%wide.region_9.10_spmd, body=%wide.region_8.9_spmd.sunk | while | flops 13631490 | bytes 2540113 | solution.py:60
  92.0 0.8 iota_compare_fusion.4
  92.9 2.2 %fusion.37 = f32[1,128,256]{2,0,1:T(1,128)S(1)} fusion(pred[32,128,256]{2,1,0:T(32,128)(4,1)S(1)} %iota_compare_fusion.4, f32[4,32]{1,0:T(4,128)S(1)} %get-tuple-element.172, s32[]{:T(128)} %get-tuple-element.163), kind=kOutput, calls=%fused_computation.6.clone.1 | convolution fusion | flops 12582912 | bytes 1180164 | tf_op jit(solution)/shard_map/while/body/eval_jaxpr/cmk,c->mk/dot_general | solution.py:56
  95.1 1.8 dynamic_update_slice.11
  97.0 0.9 iota_compare_fusion.4
  97.8 2.2 %fusion.37 = f32[1,128,256]{2,0,1:T(1,128)S(1)} fusion(pred[32,128,256]{2,1,0:T(32,128)(4,1)S(1)} %iota_compare_fusion.4, f32[4,32]{1,0:T(4,128)S(1)} %get-tuple-element.172, s32[]{:T(128)} %get-tuple-element.163), kind=kOutput, calls=%fused_computation.6.clone.1 | convolution fusion | flops 12582912 | bytes 1180164 | tf_op jit(solution)/shard_map/while/body/eval_jaxpr/cmk,c->mk/dot_general | solution.py:56
  100.0 1.8 dynamic_update_slice.11
  101.9 0.9 iota_compare_fusion.4
  102.8 2.2 %fusion.37 = f32[1,128,256]{2,0,1:T(1,128)S(1)} fusion(pred[32,128,256]{2,1,0:T(32,128)(4,1)S(1)} %iota_compare_fusion.4, f32[4,32]{1,0:T(4,128)S(1)} %get-tuple-element.172, s32[]{:T(128)} %get-tuple-element.163), kind=kOutput, calls=%fused_computation.6.clone.1 | convolution fusion | flops 12582912 | bytes 1180164 | tf_op jit(solution)/shard_map/while/body/eval_jaxpr/cmk,c->mk/dot_general | solution.py:56
  104.9 1.8 dynamic_update_slice.11
  106.8 0.9 iota_compare_fusion.4
  107.7 2.2 %fusion.37 = f32[1,128,256]{2,0,1:T(1,128)S(1)} fusion(pred[32,128,256]{2,1,0:T(32,128)(4,1)S(1)} %iota_compare_fusion.4, f32[4,32]{1,0:T(4,128)S(1)} %get-tuple-element.172, s32[]{:T(128)} %get-tuple-element.163), kind=kOutput, calls=%fused_computation.6.clone.1 | convolution fusion | flops 12582912 | bytes 1180164 | tf_op jit(solution)/shard_map/while/body/eval_jaxpr/cmk,c->mk/dot_general | solution.py:56
  109.9 1.8 dynamic_update_slice.11
  111.7 1.4 convolution_bitcast_fusion
  113.1 1.3 copy.132
  114.5 55.9 %reduce-scatter.3.cloned.1.call-done = f32[16,1024]{1,0:T(8,128)} async-done(((f32[256,1024]{1,0:T(8,128)}), f32[16,1024]{1,0:T(8,128)}) %reduce-scatter.3.cloned.1.call-update) | async-done | bytes 65552 | tf_op jit(solution)/shard_map/reduce_scatter | solution.py:108
  170.5 11.7 %reduce-scatter.5.cloned.1.call-done = f32[16,512]{1,0:T(8,128)} async-done(((f32[16,1024]{1,0:T(8,128)}), f32[16,512]{1,0:T(8,128)}) %reduce-scatter.5.cloned.1.call-update) | async-done | bytes 32784 | tf_op jit(solution)/shard_map/reduce_scatter | solution.py:109
  (53 shorter events, 1.8 us)
Async XLA Ops:
  7.2 36.7 %copy-start = (f32[128,1024]{1,0:T(8,128)S(1)}, f32[128,1024]{1,0:T(8,128)}, u32[]{:S(2)}) copy-start(f32[128,1024]{1,0:T(8,128)} %param.12) | copy-start | bytes 1572868
  7.2 36.2 %copy-start.3 = (f32[4,1024]{1,0:T(4,128)S(1)}, f32[4,1024]{1,0:T(4,128)}, u32[]{:S(2)}) copy-start(f32[4,1024]{1,0:T(4,128)} %param.11) | copy-start | bytes 49156
  7.2 36.4 %copy-start.1 = (f32[256,1024]{1,0:T(8,128)S(1)}, f32[256,1024]{1,0:T(8,128)}, u32[]{:S(2)}) copy-start(f32[256,1024]{1,0:T(8,128)} %param.14) | copy-start | bytes 3145732
  39.8 10.4 %all-to-all-start.3 = ((f32[2,16,4,128]{3,2,0,1:T(4,128)}), f32[2,16,4,128]{3,2,0,1:T(4,128)S(1)}, u32[]{:S(2)}, u32[]{:S(2)}) async-start(f32[2,16,4,128]{3,2,0,1:T(4,128)} %copy.109), calls=%async_computation.3 | async-start | bytes 131072 | tf_op jit(solution)/shard_map/all_to_all | solution.py:95
  50.2 11.5 %all-to-all-start.4 = ((f32[2,16,4,1024]{3,2,1,0:T(4,128)}), f32[2,16,4,1024]{3,2,1,0:T(4,128)S(1)}, u32[]{:S(2)}, u32[]{:S(2)}) async-start(f32[2,16,4,1024]{3,2,1,0:T(4,128)} %reshape.118), calls=%async_computation.4 | async-start | bytes 1048576 | tf_op jit(solution)/shard_map/all_to_all | solution.py:94
  71.3 18.0 %all-to-all-start.5 = ((f32[16,2,1,4,1024]{4,3,1,2,0:T(4,128)}), f32[16,2,1,4,1024]{4,3,1,2,0:T(4,128)S(1)}, u32[]{:S(2)}, u32[]{:S(2)}) async-start(f32[16,2,1,4,1024]{4,3,1,2,0:T(4,128)} %fusion.8), calls=%async_computation.5 | async-start | bytes 1048576 | tf_op jit(solution)/shard_map/all_to_all | solution.py:88
  74.9 95.5 %reduce-scatter.3.cloned.1.call-start = ((), (), s32[]{:S(2)}) async-start(), calls=%async_computation.8 | async-start | bytes 1114112 | tf_op jit(solution)/shard_map/reduce_scatter | solution.py:108
  89.6 2.5 %copy-start.2 = (f32[4,128,256]{2,0,1:T(4,128)S(1)}, f32[4,128,256]{2,0,1:T(4,128)}, u32[]{:S(2)}) copy-start(f32[4,128,256]{2,0,1:T(4,128)} %custom-call.10) | copy-start | bytes 1572868
  114.4 67.8 %reduce-scatter.5.cloned.1.call-start = ((), (), s32[]{:S(2)}) async-start(), calls=%async_computation.9 | async-start | bytes 98304 | tf_op jit(solution)/shard_map/reduce_scatter | solution.py:109
Sparse Core Ops, SparseCore 0:
  114.6 55.8 reduce-scatter.2
  173.3 8.8 reduce-scatter.4
